TPU v7x, 128 devices: a whole 4x4x4 slice. The times are simulated.
128 devices in a mesh: seq: 16 (over x_lo, y, core), tp: 8 (over z, x_hi).
Axes of the slice: x: 4 (x_hi: 2, x_lo: 2; x = x_hi * 2 + x_lo), y: 4, z: 4, core: 2. Of those that a mesh axis runs over, the one named last changes fastest.
Arguments:
- selected_hidden: bfloat16 [32, 104, 2048], P('seq', None, 'tp'), may hold values from -6 to 6
- cached_keys: bfloat16 [32, 1024, 1024], P('seq', None, 'tp'), may hold values from -48 to 48
- cached_values: bfloat16 [32, 1024, 1024], P('seq', None, 'tp'), may hold values from -6 to 6
- slot_spans: int32 [32], replicated, may hold values from 0 to 31, each once
- span_order: int32 [4, 8], replicated, may hold values from 0 to 7, each once within a row
- cache_start: int32 [4, 8], replicated, may hold values from 0 to 16383
- selected_index: int32 [32, 104], replicated, may hold values from 0 to 1023, as said below
- input_gain: bfloat16 [2048], replicated, may hold values from 0.5 to 2
- query_weight: bfloat16 [2048, 2048], P(None, 'tp'), may hold values from -0.125 to 0.125
- key_weight: bfloat16 [2048, 1024], P(None, 'tp'), may hold values from -0.125 to 0.125
- value_weight: bfloat16 [2048, 1024], P(None, 'tp'), may hold values from -0.125 to 0.125
- query_gain: bfloat16 [128], replicated, may hold values from 1 to 2
- key_gain: bfloat16 [128], replicated, may hold values from 1 to 2
- output_weight: bfloat16 [2048, 2048], P('tp'), may hold values from -0.125 to 0.125
- post_gain: bfloat16 [2048], replicated, may hold values from 0.5 to 2
- gate_weight: bfloat16 [2048, 6144], P(None, 'tp'), may hold values from -0.125 to 0.125
- up_weight: bfloat16 [2048, 6144], P(None, 'tp'), may hold values from -0.125 to 0.125
- down_weight: bfloat16 [6144, 2048], P('tp'), may hold values from -0.078125 to 0.078125
Outputs:
- new_hidden: bfloat16 [32, 104, 2048], P('seq', None, 'tp')
Inputs may be any that keep to these rules, and one draw needn't show every extreme that they name: `selected_index`: each row holds 104 distinct positions in increasing order. `slot_spans`: each span of each request is held by exactly one slot. `span_order`: each row places the 8 spans of a request in some order.
All inputs are finite; a program needn't handle non-finite values.
Results may differ from a plain program's by a relative error of at most 0.027.
Values may be sent and summed in bfloat16 or wider, within the bound.
No kernel may reach another device: no remote copies, remote signals or barrier semaphores. Data moves between devices by JAX's collectives and lax.ppermute only.
A program may use at most 128 MiB of HBM per device.

v0:
```python
import jax
import jax.numpy as jnp
from jax import lax
from jax.sharding import PartitionSpec as P

theta_base = 1000000.0
norm_eps = 1e-06


def rms_scale(values):
    return values * lax.rsqrt(jnp.mean(values * values, axis=-1, keepdims=True) + norm_eps)


def rotary(values, positions):
    half_len = values.shape[-1] // 2
    frequency = jnp.exp(
        -jnp.log(theta_base) * jnp.arange(half_len, dtype=jnp.float32) * 2.0 / values.shape[-1]
    )
    angles = positions.astype(jnp.float32)[..., None] * frequency
    cosine = jnp.cos(angles)[..., None, :]
    sine_part = jnp.sin(angles)[..., None, :]
    lower_half = values[..., :half_len]
    upper_half = values[..., half_len:]
    return jnp.concatenate(
        [
            lower_half * cosine - upper_half * sine_part,
            upper_half * cosine + lower_half * sine_part,
        ],
        axis=-1,
    )


def slot_table(slot_ids, slot_spans, span_order, cache_start, span_len):
    slot_count = slot_spans.shape[0]
    span_count = span_order.shape[1]
    slot_match = (slot_ids[:, None] == jnp.arange(slot_count, dtype=jnp.int32)[None, :]).astype(
        jnp.int32
    )
    span_ids = jnp.sum(slot_match * slot_spans[None, :], axis=1)
    span_match = (
        span_ids[:, None] == jnp.arange(span_order.size, dtype=jnp.int32)[None, :]
    ).astype(jnp.int32)
    new_place = jnp.sum(span_match * span_order.reshape(-1)[None, :], axis=1)
    old_start = jnp.sum(span_match * cache_start.reshape(-1)[None, :], axis=1)
    return (span_ids // span_count, new_place * span_len, old_start)


def on_device(
    selected_hidden,
    cached_keys,
    cached_values,
    slot_spans,
    span_order,
    cache_start,
    selected_index,
    input_gain,
    query_weight,
    key_weight,
    value_weight,
    query_gain,
    key_gain,
    output_weight,
    post_gain,
    gate_weight,
    up_weight,
    down_weight,
):
    slot_local, select_count, width_local = selected_hidden.shape
    span_len = cached_keys.shape[1]
    head_dim = query_gain.shape[0]
    kv_local = cached_keys.shape[2] // head_dim
    query_local = query_weight.shape[1] // head_dim
    group_size = query_local // kv_local
    row_count = slot_local * select_count
    score_scale = head_dim ** (-0.5)
    first_slot = lax.axis_index("seq") * slot_local
    local_slots = first_slot + jnp.arange(slot_local, dtype=jnp.int32)
    local_request, local_base, local_start = slot_table(
        local_slots, slot_spans, span_order, cache_start, span_len
    )
    local_index = lax.dynamic_slice_in_dim(selected_index, first_slot, slot_local, 0)
    query_pos = (local_base[:, None] + local_index).reshape(-1)
    query_request = jnp.broadcast_to(local_request[:, None], (slot_local, select_count)).reshape(-1)
    hidden_local = selected_hidden.reshape(row_count, width_local)
    hidden_full = lax.all_gather(hidden_local, "tp", axis=1, tiled=True)
    normed = (rms_scale(hidden_full.astype(jnp.float32)) * input_gain.astype(jnp.float32)).astype(
        jnp.bfloat16
    )
    query_proj = jnp.dot(normed, query_weight, preferred_element_type=jnp.float32).reshape(
        row_count, query_local, head_dim
    )
    queries = rotary(rms_scale(query_proj) * query_gain.astype(jnp.float32), query_pos).astype(
        jnp.bfloat16
    )
    key_proj = jnp.dot(normed, key_weight, preferred_element_type=jnp.float32).reshape(
        row_count, kv_local, head_dim
    )
    new_keys = rotary(rms_scale(key_proj) * key_gain.astype(jnp.float32), query_pos).astype(
        jnp.bfloat16
    )
    new_values = (
        jnp.dot(normed, value_weight, preferred_element_type=jnp.float32)
        .astype(jnp.bfloat16)
        .reshape(row_count, kv_local, head_dim)
    )
    shift_pos = jnp.broadcast_to((local_base - local_start)[:, None], (slot_local, span_len))
    shifted = rotary(
        cached_keys.reshape(slot_local, span_len, kv_local, head_dim).astype(jnp.float32), shift_pos
    ).astype(jnp.bfloat16)
    slot_rows = jnp.arange(slot_local, dtype=jnp.int32)[:, None]
    joined_keys = (
        shifted.at[slot_rows, local_index]
        .set(new_keys.reshape(slot_local, select_count, kv_local, head_dim))
        .reshape(slot_local, span_len, kv_local * head_dim)
    )
    joined_values = (
        cached_values.reshape(slot_local, span_len, kv_local, head_dim)
        .at[slot_rows, local_index]
        .set(new_values.reshape(slot_local, select_count, kv_local, head_dim))
        .reshape(slot_local, span_len, kv_local * head_dim)
    )

    def attend_block(state_in, query_set, key_block, value_block, slot_id):
        query_vecs, positions, requests = query_set
        key_request, key_base, unused_start = slot_table(
            slot_id[None], slot_spans, span_order, cache_start, span_len
        )
        key_pos = key_base[0] + jnp.arange(span_len, dtype=jnp.int32)
        visible = (requests[:, None] == key_request[0]) & (key_pos[None, :] <= positions[:, None])
        run_max, run_sum, run_acc = state_in
        grouped = query_vecs.reshape(-1, kv_local, group_size, head_dim)
        key_heads = key_block.reshape(span_len, kv_local, head_dim)
        value_heads = value_block.reshape(span_len, kv_local, head_dim)
        scores = (
            jnp.einsum("qkgd,lkd->qkgl", grouped, key_heads, preferred_element_type=jnp.float32)
            * score_scale
        )
        key_mask = visible[:, None, None, :]
        scores = jnp.where(key_mask, scores, -jnp.inf)
        new_max = jnp.maximum(run_max, jnp.max(scores, axis=-1))
        safe_max = jnp.where(new_max == -jnp.inf, 0.0, new_max)
        rescale = jnp.exp(run_max - safe_max)
        weights = jnp.where(key_mask, jnp.exp(scores - safe_max[..., None]), 0.0)
        new_sum = rescale * run_sum + jnp.sum(weights, axis=-1)
        new_acc = rescale[..., None] * run_acc + jnp.einsum(
            "qkgl,lkd->qkgd",
            weights.astype(jnp.bfloat16),
            value_heads,
            preferred_element_type=jnp.float32,
        )
        return (new_max, new_sum, new_acc)

    local_set = (queries, query_pos, query_request)
    piece_keys = lax.all_gather(joined_keys, "seq", axis=0, tiled=True)
    piece_values = lax.all_gather(joined_values, "seq", axis=0, tiled=True)

    def step_slot(running, slot_item):
        block_keys, block_values, offset = slot_item
        return (attend_block(running, local_set, block_keys, block_values, offset), None)

    state_out, unused_out = lax.scan(
        step_slot,
        (
            jnp.full((row_count, kv_local, group_size), -jnp.inf, jnp.float32),
            jnp.zeros((row_count, kv_local, group_size), jnp.float32),
            jnp.zeros((row_count, kv_local, group_size, head_dim), jnp.float32),
        ),
        (piece_keys, piece_values, jnp.arange(piece_keys.shape[0], dtype=jnp.int32)),
    )
    run_max, run_sum, run_acc = state_out
    attended = (run_acc / run_sum[..., None]).astype(jnp.bfloat16)
    out_part = jnp.dot(
        attended.reshape(row_count, query_local * head_dim),
        output_weight,
        preferred_element_type=jnp.float32,
    )
    attention_sum = lax.psum(out_part.astype(jnp.bfloat16), "tp").astype(jnp.float32)
    stream = (hidden_full.astype(jnp.float32) + attention_sum).astype(jnp.bfloat16)
    normed_post = (rms_scale(stream.astype(jnp.float32)) * post_gain.astype(jnp.float32)).astype(
        jnp.bfloat16
    )
    gate_values = jnp.dot(normed_post, gate_weight, preferred_element_type=jnp.float32)
    up_values = jnp.dot(normed_post, up_weight, preferred_element_type=jnp.float32)
    active = (jax.nn.silu(gate_values) * up_values).astype(jnp.bfloat16)
    feedforward_sum = lax.psum(
        jnp.dot(active, down_weight, preferred_element_type=jnp.float32).astype(jnp.bfloat16), "tp"
    ).astype(jnp.float32)
    result_full = (stream.astype(jnp.float32) + feedforward_sum).astype(jnp.bfloat16)
    result = lax.dynamic_slice_in_dim(
        result_full, lax.axis_index("tp") * width_local, width_local, 1
    )
    return result.reshape(slot_local, select_count, width_local)


def solution(mesh):
    in_specs = (
        P("seq", None, "tp"),
        P("seq", None, "tp"),
        P("seq", None, "tp"),
        P(),
        P(),
        P(),
        P(),
        P(),
        P(None, "tp"),
        P(None, "tp"),
        P(None, "tp"),
        P(),
        P(),
        P("tp", None),
        P(),
        P(None, "tp"),
        P(None, "tp"),
        P("tp", None),
    )
    out_specs = P("seq", None, "tp")
    return jax.shard_map(
        on_device, mesh=mesh, in_specs=in_specs, out_specs=out_specs, check_vma=False
    )
```

profile of v0, /device:TPU:0, one launch (start us, length us, event | category | flops | bytes accessed | tf_op | source)
XLA Modules:
  0.0 828.0 jit_solution(6008349107138852399)
XLA Ops:
  19.5 38.6 %all_gather.9 = bf16[208,2048]{1,0:T(8,128)(2,1)S(1)} all-gather(bf16[208,256]{1,0:T(8,128)(2,1)S(1)} %bitcast.112), channel_id=1, replica_groups=mesh['seq'=16,'tp'=8] {'tp'}, dimensions={1}, use_global_device_ids=true | all-gather | bytes 958464 | tf_op jit(solution)/shard_map/all_gather | solution.py:85
  60.4 21.8 %scatter_fusion = bf16[2,1024,128]{2,1,0:T(8,128)(2,1)} fusion(bf16[2,1024,128]{2,1,0:T(8,128)(2,1)} %copy.36, s32[208]{0:T(256)S(1)} %reshape.474, bf16[208,128]{1,0:T(8,128)(2,1)S(1)} %bitcast.111), kind=kCustom, calls=%fused_computation | custom fusion | bytes 161408 | tf_op jit(solution)/shard_map/scatter | solution.py:113
  84.0 21.9 %scatter_fusion.1 = bf16[2,1024,128]{2,1,0:T(8,128)(2,1)} fusion(bf16[2,1024,128]{2,1,0:T(8,128)(2,1)} %copy.64, s32[208]{0:T(256)S(1)} %reshape.474, bf16[208,128]{1,0:T(8,128)(2,1)S(1)} %convolution_convert_fusion.2), kind=kCustom, calls=%fused_computation.1 | custom fusion | bytes 161408 | tf_op jit(solution)/shard_map/scatter | solution.py:119
  106.0 2.6 fusion.63
  112.0 24.0 %all-gather.5.cloned.1.call-done = bf16[32,1024,128]{2,1,0:T(8,128)(2,1)} async-done(((bf16[2,1024,128]{2,1,0:T(8,128)(2,1)}), bf16[32,1024,128]{2,1,0:T(8,128)(2,1)}) %all-gather.5.cloned.1.call-update) | async-done | bytes 8388624 | tf_op jit(solution)/shard_map/all_gather | solution.py:154
  135.9 54.8 %all-gather.7.cloned.1.call-done = bf16[32,1024,128]{2,1,0:T(8,128)(2,1)} async-done(((bf16[2,1024,128]{2,1,0:T(8,128)(2,1)}), bf16[32,1024,128]{2,1,0:T(8,128)(2,1)}) %all-gather.7.cloned.1.call-update) | async-done | bytes 8388624 | tf_op jit(solution)/shard_map/all_gather | solution.py:155
  190.8 436.8 %while.18 = (s32[]{:T(128)}, f32[208,1,2]{0,2,1:T(2,128)S(1)}, f32[208,1,2]{0,2,1:T(2,128)S(1)}, f32[208,1,2,128]{3,0,2,1:T(8,128)}, s32[32]{0:T(128)S(1)}, /*in...) while((s32[]{:T(128)}, f32[208,1,2]{0,2,1:T(2,128)S(1)}, ...), condition=%wide.wide.region_13.14_spmd.clone, body=%wide.wide.region_8.13_spmd.clone.sunk | while | flops 222529680 | bytes 15580799 | solution.py:161
  197.4 2.6 fusion.101
  200.0 2.1 fusion.104
  211.0 2.6 fusion.101
  213.7 2.1 fusion.104
  224.7 2.6 fusion.101
  227.3 2.1 fusion.104
  238.3 2.6 fusion.101
  241.0 2.1 fusion.104
  252.0 2.6 fusion.101
  254.6 2.1 fusion.104
  265.6 2.6 fusion.101
  268.3 2.1 fusion.104
  279.3 2.6 fusion.101
  281.9 2.1 fusion.104
  292.9 2.6 fusion.101
  295.6 2.1 fusion.104
  306.6 2.6 fusion.101
  309.2 2.1 fusion.104
  320.2 2.6 fusion.101
  322.9 2.1 fusion.104
  333.9 2.6 fusion.101
  336.5 2.1 fusion.104
  347.5 2.6 fusion.101
  350.2 2.1 fusion.104
  361.2 2.6 fusion.101
  363.8 2.1 fusion.104
  374.8 2.6 fusion.101
  377.5 2.1 fusion.104
  388.5 2.6 fusion.101
  391.1 2.1 fusion.104
  402.1 2.6 fusion.101
  404.8 2.1 fusion.104
  415.8 2.6 fusion.101
  418.4 2.1 fusion.104
  429.4 2.6 fusion.101
  432.1 2.1 fusion.104
  443.1 2.6 fusion.101
  456.7 2.6 fusion.101
  470.4 2.6 fusion.101
  484.0 2.6 fusion.101
  497.7 2.6 fusion.101
  511.3 2.6 fusion.101
  525.0 2.6 fusion.101
  538.6 2.6 fusion.101
  552.3 2.6 fusion.101
  565.9 2.6 fusion.101
  579.6 2.6 fusion.101
  593.2 2.6 fusion.101
  595.9 2.1 fusion.104
  606.9 2.6 fusion.101
  620.5 2.6 fusion.101
  628.8 2.5 convolution_convert_fusion.1
  631.4 89.7 %all-reduce.3.cloned.1.call-done = bf16[208,2048]{1,0:T(8,128)(2,1)} async-done(((bf16[208,2048]{1,0:T(8,128)(2,1)}), bf16[208,2048]{1,0:T(8,128)(2,1)}) %all-reduce.3.cloned.1.call-update) | async-done | bytes 851984 | tf_op jit(solution)/shard_map/psum | solution.py:177
  721.1 3.0 multiply_reduce_fusion
  724.1 3.7 fusion.58
  727.8 5.3 convolution_convert_fusion
  733.1 86.7 %all-reduce.5.cloned.1.call-done = bf16[208,2048]{1,0:T(8,128)(2,1)} async-done(((bf16[208,2048]{1,0:T(8,128)(2,1)}), bf16[208,2048]{1,0:T(8,128)(2,1)}) %all-reduce.5.cloned.1.call-update) | async-done | bytes 851984 | tf_op jit(solution)/shard_map/psum | solution.py:185
  (702 shorter events, 238.5 us)
Async XLA Ops:
  6.5 721.2 %copy-start = (bf16[768,2048]{1,0:T(8,128)(2,1)S(1)}, bf16[768,2048]{1,0:T(8,128)(2,1)}, u32[]{:S(2)}) copy-start(bf16[768,2048]{1,0:T(8,128)(2,1)} %param.37) | copy-start | bytes 9437188
  6.5 129.4 %all-gather.5.cloned.1.call-start = ((), (), s32[]{:S(2)}) async-start(), calls=%async_computation.2 | async-start | bytes 8912896 | tf_op jit(solution)/shard_map/all_gather | solution.py:154
  12.6 97.5 %copy-start.11 = (s32[2,104]{1,0:T(2,128)}, s32[2,104]{1,0:T(2,128)S(1)}, u32[]{:S(2)}) copy-start(s32[2,104]{1,0:T(2,128)S(1)} %get-tuple-element.392) | copy-start | bytes 2500
  15.8 3.7 copy-start.7
  16.5 41.6 %copy-start.9 = (bf16[2048]{0:T(1024)(128)(2,1)S(1)}, bf16[2048]{0:T(1024)(128)(2,1)}, u32[]{:S(2)}) copy-start(bf16[2048]{0:T(1024)(128)(2,1)} %param.27) | copy-start | bytes 12292
  16.5 41.9 %copy-start.13 = (bf16[128]{0:T(256)(128)(2,1)S(1)}, bf16[128]{0:T(256)(128)(2,1)}, u32[]{:S(2)}) copy-start(bf16[128]{0:T(256)(128)(2,1)} %param.32) | copy-start | bytes 772
  19.5 39.5 %copy-start.12 = (bf16[2048,128]{1,0:T(8,128)(2,1)S(1)}, bf16[2048,128]{1,0:T(8,128)(2,1)}, u32[]{:S(2)}) copy-start(bf16[2048,128]{1,0:T(8,128)(2,1)} %param.29) | copy-start | bytes 1572868
  82.2 23.8 %copy-start.14 = (bf16[128]{0:T(256)(128)(2,1)S(1)}, bf16[128]{0:T(256)(128)(2,1)}, u32[]{:S(2)}) copy-start(bf16[128]{0:T(256)(128)(2,1)} %param.31) | copy-start | bytes 772
  82.2 108.6 %all-gather.7.cloned.1.call-start = ((), (), s32[]{:S(2)}) async-start(), calls=%async_computation.3 | async-start | bytes 8912896 | tf_op jit(solution)/shard_map/all_gather | solution.py:155
  105.9 615.2 %all-reduce.3.cloned.1.call-start = ((), (), s32[]{:S(2)}) async-start(), calls=%async_computation | async-start | bytes 1703936 | tf_op jit(solution)/shard_map/psum | solution.py:177
  108.6 82.1 %copy-start.8 = (s32[4,8]{1,0:T(4,128)S(1)}, s32[4,8]{1,0:T(4,128)}, u32[]{:S(2)}) copy-start(s32[4,8]{1,0:T(4,128)} %param.24) | copy-start | bytes 388
  108.6 82.1 %copy-start.15 = (s32[32]{0:T(128)S(1)}, s32[32]{0:T(128)}, u32[]{:S(2)}) copy-start(s32[32]{0:T(128)} %param.23) | copy-start | bytes 388
  200.0 2.2 copy-start.1
  200.0 2.2 copy-start.5
  213.6 2.2 copy-start.1
  213.6 2.2 copy-start.5
  227.3 2.2 copy-start.1
  227.3 2.2 copy-start.5
  240.9 2.2 copy-start.1
  240.9 2.2 copy-start.5
  254.6 2.2 copy-start.1
  254.6 2.2 copy-start.5
  268.2 2.2 copy-start.1
  268.2 2.2 copy-start.5
  281.9 2.2 copy-start.1
  281.9 2.2 copy-start.5
  295.5 2.2 copy-start.1
  295.5 2.2 copy-start.5
  309.2 2.2 copy-start.1
  309.2 2.2 copy-start.5
  322.8 2.2 copy-start.1
  322.8 2.2 copy-start.5
  336.5 2.2 copy-start.1
  336.5 2.2 copy-start.5
  350.1 2.2 copy-start.1
  350.1 2.2 copy-start.5
  363.8 2.2 copy-start.1
  363.8 2.2 copy-start.5
  377.4 2.2 copy-start.1
  377.4 2.2 copy-start.5
  391.1 2.2 copy-start.5
  404.7 2.2 copy-start.5
  418.4 2.2 copy-start.5
  432.0 2.2 copy-start.5
  445.7 2.2 copy-start.5
  459.3 2.2 copy-start.5
  473.0 2.2 copy-start.5
  486.7 2.2 copy-start.5
  500.3 2.2 copy-start.5
  513.9 2.2 copy-start.1
  514.0 2.2 copy-start.5
  527.6 2.2 copy-start.5
  541.3 2.2 copy-start.5
  554.9 2.2 copy-start.1
  554.9 2.2 copy-start.5
  568.6 2.2 copy-start.5
  582.2 2.2 copy-start.5
  595.9 2.2 copy-start.5
  609.5 2.2 copy-start.5
  623.2 2.2 copy-start.5
  627.6 3.8 copy-start.10
  631.3 188.5 %all-reduce.5.cloned.1.call-start = ((), (), s32[]{:S(2)}) async-start(), calls=%async_computation.1 | async-start | bytes 1703936 | tf_op jit(solution)/shard_map/psum | solution.py:185
  721.1 3.0 copy-start.3
  721.1 3.0 copy-start.4
  (49 other events, 57.7 us)
Sparse Core Ops, SparseCore 0:
  82.3 53.5 all-gather.4
  137.7 53.0 all-gather.6
  631.4 89.5 all-reduce.2
  733.2 86.5 all-reduce.4
where the time goes:
time: 833 us; the launch traced here: 828 us
  waiting for transfers between devices  255 us (31%)
  other arithmetic  173 us (21%)
  matrix products  149 us (18%)
  local copies, waits for them, and re-layouts  101 us (12%)
  loops' own time  96.9 us (12%)
  blocking collectives  38.6 us (5%)
  between operations  13.4 us (2%)
    another operation x1, loops' own time, on_device(): lax.scan(step_slot, (jnp.full((row_count, kv_local, group_size), -jnp.inf...  96.9 us
    psum x1, waiting for transfers between devices, on_device(): lax.psum(out_part.astype(jnp.bfloat16), 'tp').astype(jnp.float32)  89.7 us
    psum x1, waiting for transfers between devices, on_device(): lax.psum(jnp.dot(active, down_weight, preferred_element_type=jnp.float32)...  86.7 us
    dot_general x32, matrix products, attend_block(): jnp.einsum('qkgd,lkd->qkgl', grouped, key_heads, preferred_element_type=j...  84.1 us
    reduce_sum x32, other arithmetic, attend_block(): new_sum = rescale * run_sum + jnp.sum(weights, axis=-1)  68.4 us
    all_gather x1, waiting for transfers between devices, on_device(): piece_values = lax.all_gather(joined_values, 'seq', axis=0, tiled=True)  54.8 us
    dot_general x32, matrix products, attend_block(): jnp.einsum('qkgl,lkd->qkgd', weights.astype(jnp.bfloat16), value_heads, p...  48.8 us
    reduce_sum x33, other arithmetic, slot_table(): span_ids = jnp.sum(slot_match * slot_spans[None, :], axis=1)  42.8 us
  transfers between devices with their start and end apart: 4, of which 4 were waited for; matrix products, arithmetic and copies ran while one was open for 4% of the time, Pallas kernels for 0%

commit v1 on v0

--- a/solution.py
+++ b/solution.py
@@ -174,7 +174,9 @@
         output_weight,
         preferred_element_type=jnp.float32,
     )
-    attention_sum = lax.psum(out_part.astype(jnp.bfloat16), "tp").astype(jnp.float32)
+    attention_sum = jnp.sum(lax.all_gather(out_part.astype(jnp.bfloat16), "tp"), axis=0).astype(
+        jnp.float32
+    )
     stream = (hidden_full.astype(jnp.float32) + attention_sum).astype(jnp.bfloat16)
     normed_post = (rms_scale(stream.astype(jnp.float32)) * post_gain.astype(jnp.float32)).astype(
         jnp.bfloat16

time: 833 us -> 843 us (1.012)
    all_gather x0 -> x1, waiting for transfers between devices: none -> 94.3 us  [on_device(): lax.all_gather(out_part.astype(jnp.bfloat16), 'tp')]
    psum x1 -> x0, waiting for transfers between devices: 89.7 us -> none  [on_device(): lax.psum(out_part.astype(jnp.bfloat16), 'tp').astype(jnp.float32)]
where the time goes in v1:
time: 843 us; the launch traced here: 838 us
  waiting for transfers between devices  260 us (31%)
  other arithmetic  178 us (21%)
  matrix products  149 us (18%)
  local copies, waits for them, and re-layouts  101 us (12%)
  loops' own time  96.9 us (11%)
  blocking collectives  38.6 us (5%)
  between operations  13.4 us (2%)
    another operation x1, loops' own time, on_device(): lax.scan(step_slot, (jnp.full((row_count, kv_local, group_size), -jnp.inf...  96.9 us
    all_gather x1, waiting for transfers between devices, on_device(): lax.all_gather(out_part.astype(jnp.bfloat16), 'tp')  94.3 us
    psum x1, waiting for transfers between devices, on_device(): lax.psum(jnp.dot(active, down_weight, preferred_element_type=jnp.float32)...  86.6 us
    dot_general x32, matrix products, attend_block(): jnp.einsum('qkgd,lkd->qkgl', grouped, key_heads, preferred_element_type=j...  84.1 us
    reduce_sum x32, other arithmetic, attend_block(): new_sum = rescale * run_sum + jnp.sum(weights, axis=-1)  68.4 us
    all_gather x1, waiting for transfers between devices, on_device(): piece_values = lax.all_gather(joined_values, 'seq', axis=0, tiled=True)  54.8 us
    dot_general x32, matrix products, attend_block(): jnp.einsum('qkgl,lkd->qkgd', weights.astype(jnp.bfloat16), value_heads, p...  48.8 us
    reduce_sum x33, other arithmetic, slot_table(): span_ids = jnp.sum(slot_match * slot_spans[None, :], axis=1)  42.8 us
  transfers between devices with their start and end apart: 4, of which 4 were waited for; matrix products, arithmetic and copies ran while one was open for 4% of the time, Pallas kernels for 0%

profile of v1, /device:TPU:0, one launch (start us, length us, event | category | flops | bytes accessed | tf_op | source)
XLA Modules:
  0.0 838.1 jit_solution(12220243037394484109)
XLA Ops:
  19.5 38.6 %all_gather.15 = bf16[208,2048]{1,0:T(8,128)(2,1)S(1)} all-gather(bf16[208,256]{1,0:T(8,128)(2,1)S(1)} %bitcast.114), channel_id=1, replica_groups=mesh['seq'=16,'tp'=8] {'tp'}, dimensions={1}, use_global_device_ids=true | all-gather | bytes 958464 | tf_op jit(solution)/shard_map/all_gather | solution.py:85
  60.4 21.8 %scatter_fusion = bf16[2,1024,128]{2,1,0:T(8,128)(2,1)} fusion(bf16[2,1024,128]{2,1,0:T(8,128)(2,1)} %copy.36, s32[208]{0:T(256)S(1)} %reshape.474, bf16[208,128]{1,0:T(8,128)(2,1)S(1)} %bitcast.113), kind=kCustom, calls=%fused_computation | custom fusion | bytes 161408 | tf_op jit(solution)/shard_map/scatter | solution.py:113
  84.0 21.9 %scatter_fusion.1 = bf16[2,1024,128]{2,1,0:T(8,128)(2,1)} fusion(bf16[2,1024,128]{2,1,0:T(8,128)(2,1)} %copy.63, s32[208]{0:T(256)S(1)} %reshape.474, bf16[208,128]{1,0:T(8,128)(2,1)S(1)} %convolution_convert_fusion.2), kind=kCustom, calls=%fused_computation.1 | custom fusion | bytes 161408 | tf_op jit(solution)/shard_map/scatter | solution.py:119
  106.0 2.6 fusion.63
  111.9 24.0 %all-gather.7.cloned.1.call-done = bf16[32,1024,128]{2,1,0:T(8,128)(2,1)} async-done(((bf16[2,1024,128]{2,1,0:T(8,128)(2,1)}), bf16[32,1024,128]{2,1,0:T(8,128)(2,1)}) %all-gather.7.cloned.1.call-update) | async-done | bytes 8388624 | tf_op jit(solution)/shard_map/all_gather | solution.py:154
  135.9 54.8 %all-gather.9.cloned.1.call-done = bf16[32,1024,128]{2,1,0:T(8,128)(2,1)} async-done(((bf16[2,1024,128]{2,1,0:T(8,128)(2,1)}), bf16[32,1024,128]{2,1,0:T(8,128)(2,1)}) %all-gather.9.cloned.1.call-update) | async-done | bytes 8388624 | tf_op jit(solution)/shard_map/all_gather | solution.py:155
  190.7 436.8 %while.18 = (s32[]{:T(128)}, f32[208,1,2]{0,2,1:T(2,128)S(1)}, f32[208,1,2]{0,2,1:T(2,128)S(1)}, f32[208,1,2,128]{3,0,2,1:T(8,128)}, s32[32]{0:T(128)S(1)}, /*in...) while((s32[]{:T(128)}, f32[208,1,2]{0,2,1:T(2,128)S(1)}, ...), condition=%wide.wide.region_13.14_spmd.clone, body=%wide.wide.region_8.13_spmd.clone.sunk | while | flops 222529680 | bytes 15580799 | solution.py:161
  197.3 2.6 fusion.101
  200.0 2.1 fusion.104
  211.0 2.6 fusion.101
  213.7 2.1 fusion.104
  224.7 2.6 fusion.101
  227.3 2.1 fusion.104
  238.3 2.6 fusion.101
  241.0 2.1 fusion.104
  252.0 2.6 fusion.101
  254.6 2.1 fusion.104
  265.6 2.6 fusion.101
  268.3 2.1 fusion.104
  279.3 2.6 fusion.101
  281.9 2.1 fusion.104
  292.9 2.6 fusion.101
  295.6 2.1 fusion.104
  306.6 2.6 fusion.101
  309.2 2.1 fusion.104
  320.2 2.6 fusion.101
  322.9 2.1 fusion.104
  333.9 2.6 fusion.101
  336.5 2.1 fusion.104
  347.5 2.6 fusion.101
  350.2 2.1 fusion.104
  361.2 2.6 fusion.101
  363.8 2.1 fusion.104
  374.8 2.6 fusion.101
  377.5 2.1 fusion.104
  388.5 2.6 fusion.101
  391.1 2.1 fusion.104
  402.1 2.6 fusion.101
  404.8 2.1 fusion.104
  415.8 2.6 fusion.101
  418.4 2.1 fusion.104
  429.4 2.6 fusion.101
  443.1 2.6 fusion.101
  456.7 2.6 fusion.101
  470.4 2.6 fusion.101
  484.0 2.6 fusion.101
  497.7 2.6 fusion.101
  511.3 2.6 fusion.101
  525.0 2.6 fusion.101
  538.6 2.6 fusion.101
  541.3 2.1 fusion.104
  552.3 2.6 fusion.101
  565.9 2.6 fusion.101
  579.6 2.6 fusion.101
  593.2 2.6 fusion.101
  606.9 2.6 fusion.101
  620.5 2.6 fusion.101
  628.7 2.5 convolution_convert_fusion.1
  631.6 94.3 %all-gather.11.cloned.1.call-done = bf16[1664,2048]{1,0:T(8,128)(2,1)} async-done(((bf16[208,2048]{1,0:T(8,128)(2,1)}), bf16[1664,2048]{1,0:T(8,128)(2,1)}) %all-gather.11.cloned.1.call-update) | async-done | bytes 6815760 | tf_op jit(solution)/shard_map/all_gather | solution.py:177
  725.9 5.4 reduce_sum.112
  731.3 3.0 multiply_reduce_fusion
  734.3 3.7 fusion.58
  738.0 5.3 convolution_convert_fusion
  743.3 86.6 %all-reduce.2.cloned.1.call-done = bf16[208,2048]{1,0:T(8,128)(2,1)} async-done(((bf16[208,2048]{1,0:T(8,128)(2,1)}), bf16[208,2048]{1,0:T(8,128)(2,1)}) %all-reduce.2.cloned.1.call-update) | async-done | bytes 851984 | tf_op jit(solution)/shard_map/psum | solution.py:187
  (703 shorter events, 240.8 us)
Async XLA Ops:
  6.5 731.5 %copy-start = (bf16[768,2048]{1,0:T(8,128)(2,1)S(1)}, bf16[768,2048]{1,0:T(8,128)(2,1)}, u32[]{:S(2)}) copy-start(bf16[768,2048]{1,0:T(8,128)(2,1)} %param.37) | copy-start | bytes 9437188
  6.5 129.4 %all-gather.7.cloned.1.call-start = ((), (), s32[]{:S(2)}) async-start(), calls=%async_computation.1 | async-start | bytes 8912896 | tf_op jit(solution)/shard_map/all_gather | solution.py:154
  12.6 97.5 %copy-start.11 = (s32[2,104]{1,0:T(2,128)}, s32[2,104]{1,0:T(2,128)S(1)}, u32[]{:S(2)}) copy-start(s32[2,104]{1,0:T(2,128)S(1)} %get-tuple-element.392) | copy-start | bytes 2500
  15.8 3.7 copy-start.7
  16.5 41.6 %copy-start.9 = (bf16[2048]{0:T(1024)(128)(2,1)S(1)}, bf16[2048]{0:T(1024)(128)(2,1)}, u32[]{:S(2)}) copy-start(bf16[2048]{0:T(1024)(128)(2,1)} %param.27) | copy-start | bytes 12292
  16.5 41.9 %copy-start.13 = (bf16[128]{0:T(256)(128)(2,1)S(1)}, bf16[128]{0:T(256)(128)(2,1)}, u32[]{:S(2)}) copy-start(bf16[128]{0:T(256)(128)(2,1)} %param.32) | copy-start | bytes 772
  19.5 39.5 %copy-start.12 = (bf16[2048,128]{1,0:T(8,128)(2,1)S(1)}, bf16[2048,128]{1,0:T(8,128)(2,1)}, u32[]{:S(2)}) copy-start(bf16[2048,128]{1,0:T(8,128)(2,1)} %param.29) | copy-start | bytes 1572868
  82.2 23.8 %copy-start.14 = (bf16[128]{0:T(256)(128)(2,1)S(1)}, bf16[128]{0:T(256)(128)(2,1)}, u32[]{:S(2)}) copy-start(bf16[128]{0:T(256)(128)(2,1)} %param.31) | copy-start | bytes 772
  82.2 108.6 %all-gather.9.cloned.1.call-start = ((), (), s32[]{:S(2)}) async-start(), calls=%async_computation.2 | async-start | bytes 8912896 | tf_op jit(solution)/shard_map/all_gather | solution.py:155
  105.9 620.0 %all-gather.11.cloned.1.call-start = ((), (), s32[]{:S(2)}) async-start(), calls=%async_computation.3 | async-start | bytes 7667712 | tf_op jit(solution)/shard_map/all_gather | solution.py:177
  108.6 82.1 %copy-start.8 = (s32[4,8]{1,0:T(4,128)S(1)}, s32[4,8]{1,0:T(4,128)}, u32[]{:S(2)}) copy-start(s32[4,8]{1,0:T(4,128)} %param.24) | copy-start | bytes 388
  108.6 82.1 %copy-start.15 = (s32[32]{0:T(128)S(1)}, s32[32]{0:T(128)}, u32[]{:S(2)}) copy-start(s32[32]{0:T(128)} %param.23) | copy-start | bytes 388
  200.0 2.2 copy-start.1
  200.0 2.2 copy-start.5
  213.6 2.2 copy-start.1
  213.6 2.2 copy-start.5
  227.3 2.2 copy-start.1
  227.3 2.2 copy-start.5
  240.9 2.2 copy-start.1
  240.9 2.2 copy-start.5
  254.6 2.2 copy-start.1
  254.6 2.2 copy-start.5
  268.2 2.2 copy-start.1
  268.2 2.2 copy-start.5
  281.9 2.2 copy-start.1
  281.9 2.2 copy-start.5
  295.5 2.2 copy-start.1
  295.5 2.2 copy-start.5
  309.2 2.2 copy-start.1
  309.2 2.2 copy-start.5
  322.8 2.2 copy-start.1
  322.8 2.2 copy-start.5
  336.5 2.2 copy-start.1
  336.5 2.2 copy-start.5
  350.1 2.2 copy-start.1
  350.1 2.2 copy-start.5
  363.8 2.2 copy-start.1
  363.8 2.2 copy-start.5
  377.4 2.2 copy-start.1
  377.4 2.2 copy-start.5
  391.1 2.2 copy-start.5
  404.7 2.2 copy-start.5
  418.4 2.2 copy-start.5
  432.0 2.2 copy-start.5
  445.7 2.2 copy-start.5
  459.3 2.2 copy-start.1
  459.3 2.2 copy-start.5
  473.0 2.2 copy-start.5
  486.6 2.2 copy-start.5
  500.3 2.2 copy-start.1
  500.3 2.2 copy-start.5
  513.9 2.2 copy-start.5
  527.6 2.2 copy-start.5
  541.2 2.2 copy-start.5
  554.9 2.2 copy-start.5
  568.5 2.2 copy-start.5
  582.2 2.2 copy-start.5
  595.8 2.2 copy-start.5
  609.5 2.2 copy-start.5
  623.1 2.2 copy-start.5
  627.6 4.0 copy-start.10
  631.3 198.6 %all-reduce.2.cloned.1.call-start = ((), (), s32[]{:S(2)}) async-start(), calls=%async_computation | async-start | bytes 1703936 | tf_op jit(solution)/shard_map/psum | solution.py:187
  731.3 3.0 copy-start.3
  731.3 3.0 copy-start.4
  (49 other events, 57.7 us)
Sparse Core Ops, SparseCore 0:
  82.3 53.6 all-gather.6
  137.6 53.0 all-gather.8
  631.4 94.3 all-gather.10
  743.4 86.4 all-reduce.1
